TPU v7x, 32 devices: a whole 2x2x4 slice. The times are simulated.
32 devices in a mesh: wide: 8 (over y, x, core), quad: 4 (over z).
Axes of the slice: x: 2, y: 2, z: 4, core: 2. Of those that a mesh axis runs over, the one named last changes fastest.
Arguments:
- basis: float32 [16, 2097152], P(None, ('wide', 'quad')), may hold values from -6 to 6
- target: float32 [2097152], P(('wide', 'quad')), may hold values from -6 to 6
- sign_bits: int32 [2097152], P(('wide', 'quad')), may hold values from 0 to 1
- samples: int32 [8192], replicated, may hold values from 0 to 2097151
- owners: int32 [8192], replicated, may hold values from 0 to 7
Outputs:
- sketch: float32 [8192, 17], P(('wide', 'quad'))
- gram: float32 [8, 16, 17], P('quad')
Inputs may be any that keep to these rules, and one draw needn't show every extreme that they name: `samples`: sampled scenarios may repeat.
All inputs are finite; a program needn't handle non-finite values.
Results may differ from a plain program's by a relative error of at most 0.0003.
Values sent between devices are 32-bit elements; how exact they have to be, the bound alone decides.
A program may use at most 128 MiB of HBM per device.

v0:
```python
import math

import jax
import jax.numpy as jnp
from jax import lax
from jax.sharding import PartitionSpec as P

GROUPS = 8


def parity_sign(first, second, nbits):
    count = jnp.zeros_like(first)
    for bit in range(nbits):
        count = count + ((first & second) >> bit) & 1
    return (1 - 2 * (count & 1)).astype(jnp.float32)


def walsh_table(order):
    nbits = order.bit_length() - 1
    line = jnp.arange(order, dtype=jnp.int32)
    return parity_sign(line[:, None], line[None, :], nbits)


def shards(basis, target, sign_bits, samples, owners):
    rows = basis.shape[1]
    block = math.isqrt(rows)
    n_wide = lax.axis_size("wide")
    n_quad = lax.axis_size("quad")
    devices = n_wide * n_quad
    my_wide = lax.axis_index("wide")
    my_quad = lax.axis_index("quad")
    my_device = my_wide * n_quad + my_quad
    total_samples = samples.shape[0]
    per_dev = total_samples // devices
    scale = 1.0 / math.sqrt(rows * devices)
    flip = (1 - 2 * sign_bits).astype(jnp.float32)
    signed = jnp.concatenate([basis, target[None, :]], axis=0) * flip[None, :]
    width = signed.shape[0]
    table = walsh_table(block)
    cube = signed.reshape(width, block, block)
    cube = jnp.einsum("kab,ac->kcb", cube, table, precision=lax.Precision.HIGHEST)
    cube = jnp.einsum("kcb,bd->kcd", cube, table, precision=lax.Precision.HIGHEST)
    local = cube.reshape(width, rows)
    quarter = total_samples // n_quad
    quad_bits = n_quad.bit_length() - 1
    wide_bits = n_wide.bit_length() - 1
    line = jnp.arange(total_samples, dtype=jnp.int32)
    inner = line // quarter
    rest = line % quarter
    slots = (rest // per_dev * n_quad + inner) * per_dev + rest % per_dev
    number = samples[slots]
    values = jnp.take(local, number % rows, axis=1)
    source, values = (number // rows, values)
    sign = parity_sign(source % n_quad, jnp.full_like(source, my_quad), quad_bits)
    shared = lax.psum_scatter(values * sign[None, :], "quad", scatter_dimension=1, tiled=True)
    second = jnp.arange(quarter, dtype=jnp.int32)
    mine = (second // per_dev * n_quad + my_quad) * per_dev + second % per_dev
    outer = samples[mine] // rows // n_quad
    wide_sign = parity_sign(outer, jnp.full_like(outer, my_wide), wide_bits)
    columns = lax.psum_scatter(
        shared * (scale * wide_sign)[None, :], "wide", scatter_dimension=1, tiled=True
    )
    sketch = columns.T
    own_groups = lax.dynamic_slice_in_dim(owners, my_device * per_dev, per_dev, 0)
    onehot = (own_groups[:, None] == jnp.arange(GROUPS, dtype=jnp.int32)[None, :]).astype(
        jnp.float32
    )
    partial_gram = jnp.einsum(
        "rg,ri,rj->gij", onehot, sketch[:, : width - 1], sketch, precision=lax.Precision.HIGHEST
    )
    partial_gram = partial_gram * (GROUPS / total_samples)
    owned = GROUPS // n_quad
    summed = lax.psum(partial_gram, ("wide", "quad"))
    gram = lax.dynamic_slice_in_dim(summed, my_quad * owned, owned, 0)
    return (sketch, gram)


def solution(mesh):
    placed = (P(None, ("wide", "quad")), P(("wide", "quad")), P(("wide", "quad")), P(), P())
    return jax.shard_map(
        shards,
        mesh=mesh,
        in_specs=placed,
        out_specs=(P(("wide", "quad"), None), P("quad", None, None)),
        check_vma=False,
    )
```

profile of v0, /device:TPU:0, one launch (start us, length us, event | category | flops | bytes accessed | tf_op | source)
XLA Modules:
  0.0 308.2 jit_solution(10460242113116470487)
XLA Ops:
  7.2 0.0 reduce-scatter.3.cloned.1.call-start
  7.2 0.1 compare_select_fusion.1
  7.4 1.1 concatenate.9
  8.4 5.4 %copy.20 = f32[2,8,256,256]{3,2,1,0:T(8,128)} copy(f32[2,8,256,256]{3,1,2,0:T(8,128)} %bitcast.26) | data formatting | bytes 8388608
  13.8 0.1 mul.137
  13.9 6.7 %fusion = f32[256,17,256]{2,0,1:T(8,128)S(1)} fusion(f32[1,256,256]{2,1,0:T(8,128)S(1)} %concatenate.9, f32[16,256,256]{2,1,0:T(8,128)} %bitcast.25, f32[256,256]{1,0:T(8,128)S(1)} %mul.137), kind=kOutput, calls=%fused_computation.4 | convolution fusion | flops 3426615296 | bytes 9175040 | tf_op jit(solution)/shard_map/kab,ac->kcb/dot_general | solution.py:41
  20.6 5.7 %fusion.3 = f32[17,256,256]{2,1,0:T(8,128)} fusion(f32[256,17,256]{2,0,1:T(8,128)S(1)} %fusion), kind=kOutput, calls=%fused_computation.7 | convolution fusion | flops 3424387072 | bytes 8912896 | tf_op jit(solution)/shard_map/kcb,bd->kcd/dot_general | solution.py:42
  26.3 18.0 %copy.18 = f32[17,256,256]{0,2,1:T(8,128)} copy(f32[17,256,256]{2,1,0:T(8,128)} %fusion.3) | data formatting | bytes 8912896 | tf_op jit(solution)/shard_map/reshape | solution.py:43
  44.3 45.5 %gather_fusion = s32[8192]{0:T(1024)S(1)} fusion(s32[8192]{0:T(1024)S(1)} %copy-done, s32[8192]{0:T(1024)S(1)} %broadcast_clamp_fusion.1), kind=kCustom, calls=%fused_computation | custom fusion | bytes 98304 | tf_op jit(solution)/shard_map/gather | solution.py:51
  89.9 0.1 compare_select_fusion
  90.0 0.1 subtract_convert_fusion.1
  90.1 38.2 %gather_fusion.1 = f32[8192,17]{1,0:T(8,128)} fusion(f32[17,65536]{0,1:T(8,128)} %bitcast.24, s32[8192]{0:T(1024)S(1)} %broadcast_clamp_fusion), kind=kCustom, calls=%fused_computation.1 | custom fusion | bytes 1146880 | tf_op jit(solution)/shard_map/jit(_take)/gather | solution.py:52
  128.3 9.7 %multiply_bitcast_fusion = f32[17,8192]{0,1:T(8,128)} fusion(f32[8192,17]{1,0:T(8,128)} %gather_fusion.1, f32[8192]{0:T(1024)S(1)} %subtract_convert_fusion.1, pred[8192]{0:T(1024)(128)(4,1)S(1)} %compare_and_fusion), kind=kLoop, calls=%fused_computation.9 | loop fusion | flops 278528 | bytes 1155072 | tf_op jit(solution)/shard_map/mul | solution.py:55
  138.0 0.0 reduce-scatter.5.cloned.1.call-start
  138.1 11.8 %gather_fusion.2 = s32[2048]{0:T(1024)S(1)} fusion(s32[8192]{0:T(1024)S(1)} %copy-done, s32[2048]{0:T(1024)S(1)} %broadcast_clamp_fusion.2), kind=kCustom, calls=%fused_computation.2 | custom fusion | bytes 24576 | tf_op jit(solution)/shard_map/gather | solution.py:58
  149.9 0.8 dynamic_slice.6
  150.7 67.0 %reduce-scatter.3.cloned.1.call-done = f32[17,2048]{0,1:T(8,128)} async-done(((f32[17,8192]{0,1:T(8,128)}), f32[17,2048]{0,1:T(8,128)}) %reduce-scatter.3.cloned.1.call-update) | async-done | bytes 139280 | tf_op jit(solution)/shard_map/reduce_scatter | solution.py:55
  217.7 2.6 broadcast_multiply_fusion
  220.3 37.1 %reduce-scatter.5.cloned.1.call-done = f32[17,256]{0,1:T(8,128)} async-done(((f32[17,2048]{0,1:T(8,128)}), f32[17,256]{0,1:T(8,128)}) %reduce-scatter.5.cloned.1.call-update) | async-done | bytes 17424 | tf_op jit(solution)/shard_map/reduce_scatter | solution.py:60
  257.4 1.6 copy.15
  259.0 1.0 copy.13
  260.0 1.2 fusion.6
  261.1 39.6 %psum.7 = f32[8,16,17]{2,0,1:T(8,128)S(1)} all-reduce(f32[8,16,17]{2,0,1:T(8,128)S(1)} %fusion.6), channel_id=1, replica_groups=mesh['wide'=8,'quad'=4] {'wide','quad'}, use_global_device_ids=true, to_apply=%region_2.3 | all-reduce | flops 2176 | bytes 17408 | tf_op jit(solution)/shard_map/psum | solution.py:73
  300.8 0.6 copy.16
  (15 shorter events, 0.2 us)
Async XLA Ops:
  7.2 37.1 %copy-start = (s32[8192]{0:T(1024)S(1)}, s32[8192]{0:T(1024)}, u32[]{:S(2)}) copy-start(s32[8192]{0:T(1024)} %param.8) | copy-start | bytes 98308
  7.2 210.5 %reduce-scatter.3.cloned.1.call-start = ((), (), s32[]{:S(2)}) async-start(), calls=%async_computation.2 | async-start | bytes 5242880 | tf_op jit(solution)/shard_map/reduce_scatter | solution.py:55
  7.3 6.4 %copy-start.1 = (s32[65536]{0:T(1024)S(1)}, s32[65536]{0:T(1024)}, u32[]{:S(2)}) copy-start(s32[65536]{0:T(1024)} %param.7) | copy-start | bytes 786436
  138.0 119.4 %reduce-scatter.5.cloned.1.call-start = ((), (), s32[]{:S(2)}) async-start(), calls=%async_computation.3 | async-start | bytes 1179648 | tf_op jit(solution)/shard_map/reduce_scatter | solution.py:60
Sparse Core Ops, SparseCore 0:
  138.2 79.5 reduce-scatter.2
  220.9 36.4 reduce-scatter.4
where the time goes:
time: 309 us; the launch traced here: 308 us
  local copies, waits for them, and re-layouts  124 us (40%)
  waiting for transfers between devices  104 us (34%)
  blocking collectives  39.6 us (13%)
  between operations  14.2 us (5%)
  matrix products  13.6 us (4%)
  other arithmetic  12.7 us (4%)
    reduce_scatter x1, waiting for transfers between devices, shards(): lax.psum_scatter(values * sign[None, :], 'quad', scatter_dimension=1, til...  67 us
    gather x1, local copies, waits for them, and re-layouts, shards(): number = samples[slots]  45.5 us
    psum x1, blocking collectives, shards(): summed = lax.psum(partial_gram, ('wide', 'quad'))  39.6 us
    gather x1, local copies, waits for them, and re-layouts, shards(): values = jnp.take(local, number % rows, axis=1)  38.2 us
    reduce_scatter x1, waiting for transfers between devices, shards(): lax.psum_scatter(shared * (scale * wide_sign)[None, :], 'wide', scatter_d...  37.1 us
    reshape x1, local copies, waits for them, and re-layouts, shards(): local = cube.reshape(width, rows)  18 us
    gather x1, local copies, waits for them, and re-layouts, shards(): outer = samples[mine] // rows // n_quad  11.8 us
    mul x1, other arithmetic, shards(): values * sign[None, :]  9.67 us
  transfers between devices with their start and end apart: 2, of which 2 were waited for; matrix products, arithmetic and copies ran while one was open for 4% of the time, Pallas kernels for 0%

commit v1 on v0

v1 whole, which is shorter than its diff:
```python
import functools
import math

import jax
import jax.numpy as jnp
from jax import lax
from jax.experimental import pallas as pl
from jax.experimental.pallas import tpu as pltpu
from jax.sharding import PartitionSpec as P

GROUPS = 8
LANES = 128
LINE = 256
HIGH = 8
SLOT = 32
MESH = pl.DeviceIdType.MESH


def bits_of(n):
    return n.bit_length() - 1


def parity(x, nbits):
    shift = 1
    while shift < nbits:
        x = x ^ (x >> shift)
        shift *= 2
    return x & 1


def butterfly(parts):
    half = 1
    while half < len(parts):
        for at in range(0, len(parts), 2 * half):
            for i in range(at, at + half):
                parts[i], parts[i + half] = parts[i] + parts[i + half], parts[i] - parts[i + half]
        half *= 2
    return parts


def place_of(high):
    return ((high & 1) * (HIGH // 2) + (high >> 1)) * SLOT


def split(x):
    top = x.astype(jnp.bfloat16)
    return top, (x - top.astype(jnp.float32)).astype(jnp.bfloat16)


def contract_last(a, b, **kw):
    return lax.dot_general(a, b, (((1,), (1,)), ((), ())), preferred_element_type=jnp.float32, **kw)


def transform_kernel(
    n_wide, n_quad, scale, picks, samp, bits, x, t, main, last, field, table, walsh, unit, picked
):
    high = pl.program_id(0)
    cols, chunk = x.shape
    mids = chunk // LINE
    local_bits = bits_of(HIGH * chunk)
    per_dev = main.shape[2]
    devices = n_wide * n_quad

    @pl.when(high == 0)
    def _():
        a = lax.broadcasted_iota(jnp.int32, (LINE, LINE), 0)
        b = lax.broadcasted_iota(jnp.int32, (LINE, LINE), 1)
        walsh[...] = (1 - 2 * parity(a & b, bits_of(LINE))).astype(jnp.float32).astype(jnp.bfloat16)
        a = lax.broadcasted_iota(jnp.int32, (LANES, LANES), 0)
        b = lax.broadcasted_iota(jnp.int32, (LANES, LANES), 1)
        unit[...] = jnp.where(a == b, 1.0, 0.0).astype(jnp.bfloat16)

    row = lax.broadcasted_iota(jnp.int32, (8, LANES), 0)
    base = pl.multiple_of(place_of(high), SLOT)
    for part in range(LINE // LANES):
        for tile in range(cols // 8 + 1):
            values = []
            for mid in range(mids):
                line = mid * (LINE // LANES) + part
                flip = (1 - 2 * bits[line : line + 1, :]).astype(jnp.float32)
                if tile < cols // 8:
                    value = x[tile * 8 : tile * 8 + 8, line * LANES : (line + 1) * LANES] * flip
                else:
                    value = jnp.where(row == 0, t[line : line + 1, :] * flip, 0.0)
                values.append(value)
            for mid, value in enumerate(butterfly(values)):
                field[mid, pl.ds(base + tile * 8, 8), part * LANES : (part + 1) * LANES] = value

    @pl.when(high == HIGH - 1)
    def _():
        used = cols + 8

        def mix(mid, carry):
            halves = []
            for part in range(LINE // LANES):
                values = [
                    field[mid, place_of(h) : place_of(h) + used, part * LANES : (part + 1) * LANES]
                    for h in range(HIGH)
                ]
                values = butterfly(values)
                order = sorted(range(HIGH), key=place_of)
                blank = jnp.zeros((SLOT - used, LANES), jnp.float32)
                halves.append(jnp.concatenate([p for h in order for p in (values[h], blank)], axis=0))
            top, low = split(jnp.concatenate(halves, axis=1))
            out = contract_last(walsh[...], top) + contract_last(walsh[...], low)
            at = pl.multiple_of(mid * LINE, LINE)
            table[pl.ds(at, LINE), :] = out[:, :LANES]
            table[pl.ds(at + mids * LINE, LINE), :] = out[:, LANES:]
            return carry

        lax.fori_loop(0, mids, mix, 0)
        me = lax.axis_index("wide") * n_quad + lax.axis_index("quad")
        table_rows = table.shape[0]

        def gather(slot, carry):
            wide = slot // n_quad
            turned = jnp.int32(0)
            for bit in range(bits_of(n_wide)):
                turned = turned * 2 + ((wide >> bit) & 1)
            dev = turned * n_quad + slot % n_quad
            start = dev * per_dev
            for r in range(per_dev):
                at = picks[start + r] & (table_rows - 1)
                picked[r : r + 1, :] = table[pl.ds(at, 1), :]
            top, low = split(picked[...])
            out = contract_last(unit[...], top) + contract_last(unit[...], low)
            lines = per_dev // LANES
            number = jnp.concatenate(
                [samp[pl.ds(dev * lines + i, 1), :] for i in range(lines)], axis=1
            )
            group = (number >> bits_of(table_rows)) & (LANES // SLOT - 1)
            sign = parity((number >> local_bits) & me, bits_of(devices))
            sign = (1 - 2 * sign).astype(jnp.float32) * scale
            total = jnp.zeros((used, per_dev), jnp.float32)
            for g in range(LANES // SLOT):
                total = jnp.where(group == g, out[g * SLOT : g * SLOT + used, :], total)
            total = total * sign
            main[slot] = total[:cols]
            for i in range(lines):
                last[pl.ds(slot * lines + i, 1), :] = total[cols : cols + 1, i * LANES : (i + 1) * LANES]
            return carry

        lax.fori_loop(0, devices, gather, 0)


def reduce_kernel(n_wide, n_quad, total_samples, main, last, owners, sketch, gram, *scratch):
    steps = bits_of(n_wide)
    got_main, scratch = scratch[:steps], scratch[steps:]
    got_last, scratch = scratch[:steps], scratch[steps:]
    sum_main, scratch = scratch[:steps], scratch[steps:]
    sum_last, scratch = scratch[:steps], scratch[steps:]
    quad_main, quad_last, gram_own, gram_got, quad_gram, turned, sends, recvs = scratch
    wide = lax.axis_index("wide")
    quad = lax.axis_index("quad")
    me = wide * n_quad + quad
    devices, cols, per_dev = main.shape
    lines = per_dev // LANES
    pairs = [(wide + (1 << k) - 2 * (1 << k) * ((wide // (1 << k)) % 2), quad) for k in range(steps)]
    rows = [(wide, (quad + k) % n_quad) for k in range(1, n_quad)]

    barrier = pltpu.get_barrier_semaphore()
    for peer in pairs + rows:
        pl.semaphore_signal(barrier, inc=1, device_id=peer, device_id_type=MESH)
    pl.semaphore_wait(barrier, len(pairs) + len(rows))

    used = [0]

    def send(src, dst, peer):
        sem = used[0]
        used[0] += 1
        copy = pltpu.make_async_remote_copy(
            src_ref=src, dst_ref=dst, send_sem=sends.at[sem], recv_sem=recvs.at[sem],
            device_id=peer, device_id_type=MESH,
        )
        copy.start()
        return copy

    now_main, now_last = main, last
    pending = []
    copies = []
    size = devices
    for k in range(steps):
        size //= 2
        bit = (wide // (1 << k)) % 2
        give, keep = (1 - bit) * size, bit * size
        if k:
            add_up(now_main, now_last, before, give, size, lines)
        copies = [
            send(now_main.at[pl.ds(give, size)], got_main[k], pairs[k]),
            send(now_last.at[pl.ds(pl.multiple_of(give * lines, 8), size * lines)], got_last[k], pairs[k]),
        ]
        if k:
            add_up(now_main, now_last, before, keep, size, lines)
        for copy in copies:
            copy.wait()
        before = (now_main, now_last, got_main[k], got_last[k], keep)
        now_main, now_last = sum_main[k], sum_last[k]
    for k in range(1, n_quad):
        add_up(now_main, now_last, before, (quad + k) % n_quad, 1, 0)
    add_up(now_main, now_last, before, 0, n_quad, lines, False)
    copies = []
    for k, peer in enumerate(rows):
        copies.append(send(now_main.at[peer[1]], quad_main.at[k], peer))
        copies.append(send(now_last, quad_last.at[k], peer))
    add_up(now_main, now_last, before, quad, 1, 0)
    for copy in copies:
        copy.wait()
    total = now_main[quad]
    ends = [now_last[pl.ds(quad * lines + i, 1), :] for i in range(lines)]
    for k in range(n_quad - 1):
        total = total + quad_main[k]
        ends = [e + quad_last[k, pl.ds(quad * lines + i, 1), :] for i, e in enumerate(ends)]
    end = jnp.concatenate(ends, axis=1)
    sketch[:cols, :] = total
    sketch[cols : cols + 1, :] = end

    group = jnp.concatenate([owners[pl.ds(me * lines + i, 1), :] for i in range(lines)], axis=1)
    row = lax.broadcasted_iota(jnp.int32, (8, per_dev), 0)
    right = jnp.concatenate([total, jnp.where(row == 0, end, 0.0)], axis=0)
    left = jnp.concatenate([jnp.where(group == g, total, 0.0) for g in range(GROUPS)], axis=0)
    part = contract_last(right, left, precision=lax.Precision.HIGHEST)
    part = part * (GROUPS / total_samples)
    for k in range(steps):
        gram_own[k] = part
        copy = send(gram_own.at[k], gram_got.at[k], pairs[k])
        copy.wait()
        part = part + gram_got[k]
    gram_own[steps] = part
    copies = [send(gram_own.at[steps], quad_gram.at[k], peer) for k, peer in enumerate(rows)]
    for copy in copies:
        copy.wait()
    for k in range(n_quad - 1):
        part = part + quad_gram[k]
    turned[:, : part.shape[0]] = part.T
    owned = GROUPS // n_quad
    for g in range(owned):
        gram[g] = turned[pl.ds((quad * owned + g) * cols, cols), : cols + 1]


def add_up(out_main, out_last, before, start, size, lines, whole=True):
    main, last, got_main, got_last, keep = before
    if whole:
        out_main[pl.ds(start, size)] = main[pl.ds(keep + start, size)] + got_main[pl.ds(start, size)]
    if lines:
        to = pl.multiple_of(start * lines, 8)
        at = pl.multiple_of((keep + start) * lines, 8)
        out_last[pl.ds(to, size * lines), :] = (
            last[pl.ds(at, size * lines), :] + got_last[pl.ds(to, size * lines), :]
        )


def shards(n_wide, n_quad, basis, target, sign_bits, samples, owners):
    cols, rows = basis.shape
    devices = n_wide * n_quad
    total_samples = samples.shape[0]
    per_dev = total_samples // devices
    lines = per_dev // LANES
    scale = 1.0 / math.sqrt(rows * devices)
    chunk = rows // HIGH
    mids = chunk // LINE
    vmem = pl.BlockSpec(memory_space=pltpu.VMEM)
    f32 = jnp.float32
    main, last = pl.pallas_call(
        functools.partial(transform_kernel, n_wide, n_quad, scale),
        grid=(HIGH,),
        out_shape=(
            jax.ShapeDtypeStruct((devices, cols, per_dev), f32),
            jax.ShapeDtypeStruct((devices * lines, LANES), f32),
        ),
        in_specs=[
            pl.BlockSpec(memory_space=pltpu.SMEM),
            vmem,
            pl.BlockSpec((chunk // LANES, LANES), lambda h: (h, 0)),
            pl.BlockSpec((cols, chunk), lambda h: (0, h)),
            pl.BlockSpec((chunk // LANES, LANES), lambda h: (h, 0)),
        ],
        out_specs=(vmem, vmem),
        scratch_shapes=[
            pltpu.VMEM((mids, HIGH * SLOT, LINE), f32),
            pltpu.VMEM((rows * SLOT // LANES, LANES), f32),
            pltpu.VMEM((LINE, LINE), jnp.bfloat16),
            pltpu.VMEM((LANES, LANES), jnp.bfloat16),
            pltpu.VMEM((per_dev, LANES), f32),
        ],
        compiler_params=pltpu.CompilerParams(vmem_limit_bytes=60 * 1024 * 1024),
    )(
        samples,
        samples.reshape(-1, LANES),
        sign_bits.reshape(-1, LANES),
        basis,
        target.reshape(-1, LANES),
    )

    steps = bits_of(n_wide)
    sizes = [devices >> (k + 1) for k in range(steps)]
    mains = [pltpu.VMEM((s, cols, per_dev), f32) for s in sizes]
    lasts = [pltpu.VMEM((s * lines, LANES), f32) for s in sizes]
    copies = 3 * steps + 3 * (n_quad - 1)
    wide_gram = GROUPS * cols
    tall = cols + 8
    sketch, gram = pl.pallas_call(
        functools.partial(reduce_kernel, n_wide, n_quad, total_samples),
        out_shape=(
            jax.ShapeDtypeStruct((cols + 1, per_dev), f32),
            jax.ShapeDtypeStruct((GROUPS // n_quad, cols, cols + 1), f32),
        ),
        in_specs=[vmem, vmem, vmem],
        out_specs=(vmem, vmem),
        scratch_shapes=mains + lasts + mains + lasts + [
            pltpu.VMEM((n_quad - 1, cols, per_dev), f32),
            pltpu.VMEM((n_quad - 1, n_quad * lines, LANES), f32),
            pltpu.VMEM((steps + 1, tall, wide_gram), f32),
            pltpu.VMEM((steps, tall, wide_gram), f32),
            pltpu.VMEM((n_quad - 1, tall, wide_gram), f32),
            pltpu.VMEM((wide_gram, LANES), f32),
            pltpu.SemaphoreType.DMA((copies,)),
            pltpu.SemaphoreType.DMA((copies,)),
        ],
        compiler_params=pltpu.CompilerParams(collective_id=0, has_side_effects=True),
    )(main, last, owners.reshape(-1, LANES))
    return sketch.T, gram


def solution(mesh):
    placed = (P(None, ("wide", "quad")), P(("wide", "quad")), P(("wide", "quad")), P(), P())
    return jax.shard_map(
        functools.partial(shards, mesh.shape["wide"], mesh.shape["quad"]),
        mesh=mesh,
        in_specs=placed,
        out_specs=(P(("wide", "quad"), None), P("quad", None, None)),
        check_vma=False,
    )
```

time: 309 us -> 65.8 us (0.21)
  local copies, waits for them, and re-layouts: 124 us -> 2.67 us
  waiting for transfers between devices: 104 us -> 0 us
  Pallas kernels: 0 us -> 62.2 us
  blocking collectives: 39.6 us -> 0 us
  matrix products: 13.6 us -> 0 us
  between operations: 14.2 us -> 0.64 us
  other arithmetic: 12.7 us -> 0 us
    reduce_scatter x2 -> x0, waiting for transfers between devices: 104 us -> none  [the longest x1 67 us: shards(): lax.psum_scatter(values * sign[None, :], 'quad', scatter_dimension=1, til...]
    gather x3 -> x0, local copies, waits for them, and re-layouts: 95.6 us -> none  [the longest x1 45.5 us: shards(): number = samples[slots]]
    pallas_call x0 -> x2, Pallas kernels: none -> 62.2 us  [the longest x1 31.1 us: shards(): pl.pallas_call(functools.partial(transform_kernel, n_wide, n_quad, scale)...]
    psum x1 -> x0, blocking collectives: 39.6 us -> none  [shards(): summed = lax.psum(partial_gram, ('wide', 'quad'))]
    reshape x1 -> x0, local copies, waits for them, and re-layouts: 18 us -> none  [shards(): local = cube.reshape(width, rows)]
    dot_general x3 -> x0, matrix products: 13.6 us -> none  [the longest x1 6.72 us: shards(): jnp.einsum('kab,ac->kcb', cube, table, precision=lax.Precision.HIGHEST)]
    mul x3 -> x0, other arithmetic: 12.3 us -> none  [the longest x1 9.67 us: shards(): values * sign[None, :]]
    unnamed x7 -> x2, local copies, waits for them, and re-layouts: 7.58 us -> 2.67 us
  transfers between devices with their start and end apart: 2 -> 0, of which waited for: 2 -> 0; matrix products, arithmetic and copies ran while one was open for 4% -> 0% of each run, Pallas kernels for 0% -> 0%
where the time goes in v1:
time: 65.8 us; the launch traced here: 65.5 us
  Pallas kernels  62.2 us (95%)
  local copies, waits for them, and re-layouts  2.67 us (4%)
    pallas_call x1, Pallas kernels, shards(): pl.pallas_call(functools.partial(transform_kernel, n_wide, n_quad, scale)...  31.1 us
    pallas_call x1, Pallas kernels, shards(): pl.pallas_call(functools.partial(reduce_kernel, n_wide, n_quad, total_sam...  31 us
    unnamed x2, local copies, waits for them, and re-layouts  2.67 us

profile of v1, /device:TPU:0, one launch (start us, length us, event | category | flops | bytes accessed | tf_op | source)
XLA Modules:
  0.0 65.5 jit_solution(3308327620455846133)
XLA Ops:
  0.6 31.1 %shard_map.68 = (f32[32,16,256]{2,1,0:T(8,128)}, f32[64,128]{1,0:T(8,128)}) custom-call(s32[8192]{0:T(1024)} %picks.1, s32[64,128]{1,0:T(8,128)} %bitcast.7, s32[512,128]{1,0:T(8,128)} %bitcast.5, f32[16,65536]{1,0:T(8,128)} %x.1, f32[512,128]{1,0:T(8,128)} %bitcast.6), custom_call_target="tpu_custom_call" | custom-call | tf_op jit(solution)/shard_map/pallas_call | solution.py:263
  31.8 31.0 %shard_map.69 = (f32[17,256]{1,0:T(8,128)}, f32[2,16,17]{2,1,0:T(8,128)}) custom-call(f32[32,16,256]{2,1,0:T(8,128)} %get-tuple-element.6.main, f32[64,128]{1,0:T(8,128)} %get-tuple-element.7.last, s32[64,128]{1,0:T(8,128)} %bitcast.8), custom_call_target="tpu_custom_call" | custom-call | tf_op jit(solution)/shard_map/pallas_call | solution.py:301
  62.8 1.3 %copy.9 = f32[256,17]{0,1:T(8,128)} copy(f32[256,17]{0,1:T(8,128)} %bitcast.9) | data formatting | bytes 34816
  64.2 1.3 %copy.10 = f32[2,16,17]{2,1,0:T(8,128)} copy(f32[2,16,17]{2,1,0:T(8,128)} %get-tuple-element.13) | data formatting | bytes 4352

commit v2 on v1

v2 whole, which is shorter than its diff:
```python
import functools
import math

import jax
import jax.numpy as jnp
from jax import lax
from jax.experimental import pallas as pl
from jax.experimental.pallas import tpu as pltpu
from jax.sharding import PartitionSpec as P

GROUPS = 8
LANES = 128
LINE = 256
HIGH = 8
SLOT = 32
MESH = pl.DeviceIdType.MESH


def bits_of(n):
    return n.bit_length() - 1


def parity(x, nbits):
    shift = 1
    while shift < nbits:
        x = x ^ (x >> shift)
        shift *= 2
    return x & 1


def butterfly(parts):
    half = 1
    while half < len(parts):
        for at in range(0, len(parts), 2 * half):
            for i in range(at, at + half):
                parts[i], parts[i + half] = parts[i] + parts[i + half], parts[i] - parts[i + half]
        half *= 2
    return parts


def place_of(high):
    return ((high & 1) * (HIGH // 2) + (high >> 1)) * SLOT


def split(x):
    top = x.astype(jnp.bfloat16)
    return top, (x - top.astype(jnp.float32)).astype(jnp.bfloat16)


def contract_last(a, b, **kw):
    return lax.dot_general(a, b, (((1,), (1,)), ((), ())), preferred_element_type=jnp.float32, **kw)


def transform_kernel(
    n_wide, n_quad, scale, samp, bits, x, t, main, last, field, table, walsh, unit,
    picks, picks_a, picks_b, rows_a, rows_b, sems
):
    high = pl.program_id(0)
    cols, chunk = x.shape
    mids = chunk // LINE
    local_bits = bits_of(HIGH * chunk)
    per_dev = main.shape[2]
    devices = n_wide * n_quad

    @pl.when(high == 0)
    def _():
        a = lax.broadcasted_iota(jnp.int32, (LINE, LINE), 0)
        b = lax.broadcasted_iota(jnp.int32, (LINE, LINE), 1)
        line = (1 - 2 * parity(a & b, bits_of(LINE))).astype(jnp.float32).astype(jnp.bfloat16)
        walsh[:, :LINE] = line
        walsh[:, LINE:] = line
        a = lax.broadcasted_iota(jnp.int32, (LANES, LANES), 0)
        b = lax.broadcasted_iota(jnp.int32, (LANES, LANES), 1)
        line = jnp.where(a == b, 1.0, 0.0).astype(jnp.bfloat16)
        unit[:, :LANES] = line
        unit[:, LANES:] = line
        picks[...] = samp[...] & (table.shape[0] - 1)

    row = lax.broadcasted_iota(jnp.int32, (8, LANES), 0)
    base = pl.multiple_of(place_of(high), SLOT)
    for part in range(LINE // LANES):
        for tile in range(cols // 8 + 1):
            values = []
            for mid in range(mids):
                line = mid * (LINE // LANES) + part
                flip = (1 - 2 * bits[line : line + 1, :]).astype(jnp.float32)
                if tile < cols // 8:
                    value = x[tile * 8 : tile * 8 + 8, line * LANES : (line + 1) * LANES] * flip
                else:
                    value = jnp.where(row == 0, t[line : line + 1, :] * flip, 0.0)
                values.append(value)
            for mid, value in enumerate(butterfly(values)):
                field[mid, pl.ds(base + tile * 8, 8), part * LANES : (part + 1) * LANES] = value

    @pl.when(high == HIGH - 1)
    def _():
        used = cols + 8

        def mix(mid, carry):
            halves = []
            for part in range(LINE // LANES):
                values = [
                    field[mid, place_of(h) : place_of(h) + used, part * LANES : (part + 1) * LANES]
                    for h in range(HIGH)
                ]
                values = butterfly(values)
                order = sorted(range(HIGH), key=place_of)
                blank = jnp.zeros((SLOT - used, LANES), jnp.float32)
                halves.append(jnp.concatenate([p for h in order for p in (values[h], blank)], axis=0))
            both = jnp.concatenate(split(jnp.concatenate(halves, axis=1)), axis=1)
            out = contract_last(walsh[...], both)
            at = pl.multiple_of(mid * LINE, LINE)
            table[pl.ds(at, LINE), :] = out[:, :LANES]
            table[pl.ds(at + mids * LINE, LINE), :] = out[:, LANES:]
            return carry

        lax.fori_loop(0, mids, mix, 0, unroll=2)
        me = lax.axis_index("wide") * n_quad + lax.axis_index("quad")
        table_rows = table.shape[0]
        lines = per_dev // LANES
        inner = devices // 2

        def device_at(slot):
            wide = (slot // n_quad) % (n_wide // 2) * 2 + slot // inner
            return wide * n_quad + slot % n_quad

        def fetch(slot, slots, sem):
            slot = jnp.minimum(slot, devices - 1)
            return pltpu.make_async_copy(picks.at[device_at(slot)], slots, sems.at[sem])

        def gather(slots, rows):
            for r in range(per_dev):
                rows[r : r + 1, :] = table[pl.ds(slots[r // LANES, r % LANES], 1), :]

        def finish(slot, rows):
            dev = device_at(slot)
            out = contract_last(unit[...], jnp.concatenate(split(rows[...]), axis=1))
            number = jnp.concatenate([samp[dev, i : i + 1] for i in range(lines)], axis=1)
            group = (number >> bits_of(table_rows)) & (LANES // SLOT - 1)
            sign = parity((number >> local_bits) & me, bits_of(devices))
            sign = (1 - 2 * sign).astype(jnp.float32) * scale
            total = jnp.zeros((used, per_dev), jnp.float32)
            for g in range(LANES // SLOT):
                total = jnp.where(group == g, out[g * SLOT : g * SLOT + used, :], total)
            total = total * sign
            main[slot] = total[:cols]
            for i in range(lines):
                last[pl.ds(slot * lines + i, 1), :] = total[cols : cols + 1, i * LANES : (i + 1) * LANES]

        fetch(0, picks_a, 0).start()
        fetch(1, picks_b, 1).start()
        fetch(0, picks_a, 0).wait()
        gather(picks_a, rows_a)
        fetch(2, picks_a, 0).start()

        def pair(i, carry):
            slot = 2 * i
            fetch(slot + 1, picks_b, 1).wait()
            gather(picks_b, rows_b)
            finish(slot, rows_a)
            fetch(slot + 3, picks_b, 1).start()
            fetch(slot + 2, picks_a, 0).wait()
            gather(picks_a, rows_a)
            finish(slot + 1, rows_b)
            fetch(slot + 4, picks_a, 0).start()
            return carry

        lax.fori_loop(0, devices // 2, pair, 0)
        fetch(0, picks_a, 0).wait()
        fetch(0, picks_b, 1).wait()


def reduce_kernel(
    n_wide, n_quad, total_samples, main, last, owners, sketch, gram,
    got_main, got_last, sum_main, sum_last, wide_main, wide_last, row_main, row_last,
    quad_main, quad_last, wide_gram, own_gram, quad_gram, sends, recvs
):
    wide = lax.axis_index("wide")
    quad = lax.axis_index("quad")
    me = wide * n_quad + quad
    devices, cols, per_dev = main.shape
    lines = per_dev // LANES
    core, chip, chips = wide % 2, wide // 2, n_wide // 2
    mate = (wide + 1 - 2 * core, quad)
    chip_peers = [(chip + k) % chips for k in range(1, chips)]
    wide_peers = [((wide + k) % n_wide, quad) for k in range(1, n_wide)]
    quad_peers = [(wide, (quad + k) % n_quad) for k in range(1, n_quad)]

    barrier = pltpu.get_barrier_semaphore()
    for peer in wide_peers + quad_peers:
        pl.semaphore_signal(barrier, inc=1, device_id=peer, device_id_type=MESH)
    pl.semaphore_wait(barrier, len(wide_peers) + len(quad_peers))

    used = [0]

    def send(src, dst, peer):
        sem = used[0]
        used[0] += 1
        copy = pltpu.make_async_remote_copy(
            src_ref=src, dst_ref=dst, send_sem=sends.at[sem], recv_sem=recvs.at[sem],
            device_id=peer, device_id_type=MESH,
        )
        copy.start()
        return copy

    half = devices // 2
    tall = n_quad * lines
    give, keep = (1 - core) * half, core * half
    copies = [
        send(main.at[pl.ds(give, half)], got_main, mate),
        send(last.at[pl.ds(pl.multiple_of(give * lines, 8), half * lines)], got_last, mate),
    ]
    for copy in copies:
        copy.wait()

    def add(to):
        at = pl.ds(to * n_quad, n_quad)
        sum_main[at] = main[pl.ds(keep + to * n_quad, n_quad)] + got_main[at]
        at = pl.ds(pl.multiple_of(to * tall, 8), tall)
        from_at = pl.ds(pl.multiple_of(keep * lines + to * tall, 8), tall)
        sum_last[at, :] = last[from_at, :] + got_last[at, :]

    copies = []
    for k, peer in enumerate(chip_peers):
        add(peer)
        there = (peer * 2 + core, quad)
        copies.append(send(sum_main.at[pl.ds(peer * n_quad, n_quad)], wide_main.at[k], there))
        copies.append(
            send(sum_last.at[pl.ds(pl.multiple_of(peer * tall, 8), tall)], wide_last.at[k], there)
        )
    add(chip)
    for copy in copies:
        copy.wait()

    def add_row(to):
        row = sum_main[chip * n_quad + to]
        for k in range(chips - 1):
            row = row + wide_main[k, to]
        row_main[to] = row

    ends = sum_last[pl.ds(pl.multiple_of(chip * tall, 8), tall), :]
    for k in range(chips - 1):
        ends = ends + wide_last[k]
    row_last[...] = ends
    copies = []
    for k, peer in enumerate(quad_peers):
        add_row(peer[1])
        copies.append(send(row_main.at[peer[1]], quad_main.at[k], peer))
        copies.append(send(row_last, quad_last.at[k], peer))
    add_row(quad)
    for copy in copies:
        copy.wait()
    total = row_main[quad]
    ends = [row_last[pl.ds(quad * lines + i, 1), :] for i in range(lines)]
    for k in range(n_quad - 1):
        total = total + quad_main[k]
        ends = [e + quad_last[k, pl.ds(quad * lines + i, 1), :] for i, e in enumerate(ends)]
    end = jnp.concatenate(ends, axis=1)
    sketch[:cols, :] = total
    sketch[cols : cols + 1, :] = end

    group = jnp.concatenate([owners[me, i : i + 1] for i in range(lines)], axis=1)
    row = lax.broadcasted_iota(jnp.int32, (8, per_dev), 0)
    right = jnp.concatenate([total, jnp.where(row == 0, end, 0.0)], axis=0)
    left = jnp.concatenate([jnp.where(group == g, total, 0.0) for g in range(GROUPS)], axis=0)
    part = contract_last(right, left, precision=lax.Precision.HIGHEST)
    wide_gram[0] = part * (GROUPS / total_samples)
    copies = [send(wide_gram.at[0], wide_gram.at[k + 1], peer) for k, peer in enumerate(wide_peers)]
    for copy in copies:
        copy.wait()
    part = wide_gram[wide]
    for w in range(1, n_wide):
        part = part + wide_gram[(wide + n_wide - w) % n_wide]
    own_gram[...] = part
    copies = [send(own_gram, quad_gram.at[k], peer) for k, peer in enumerate(quad_peers)]
    for copy in copies:
        copy.wait()
    for k in range(n_quad - 1):
        part = part + quad_gram[k]
    gram[...] = part


def finish_kernel(n_quad, sketch_in, gram_in, sketch, gram, turned):
    quad = lax.axis_index("quad")
    owned, cols, _ = gram.shape
    sketch[...] = sketch_in[...]
    turned[:, : gram_in.shape[0]] = gram_in[...].T
    for g in range(owned):
        gram[g] = turned[pl.ds((quad * owned + g) * cols, cols), : cols + 1]


def shards(n_wide, n_quad, basis, target, sign_bits, samples, owners):
    cols, rows = basis.shape
    devices = n_wide * n_quad
    total_samples = samples.shape[0]
    per_dev = total_samples // devices
    lines = per_dev // LANES
    scale = 1.0 / math.sqrt(rows * devices)
    chunk = rows // HIGH
    mids = chunk // LINE
    vmem = pl.BlockSpec(memory_space=pltpu.VMEM)
    f32 = jnp.float32
    main, last = pl.pallas_call(
        functools.partial(transform_kernel, n_wide, n_quad, scale),
        grid=(HIGH,),
        out_shape=(
            jax.ShapeDtypeStruct((devices, cols, per_dev), f32),
            jax.ShapeDtypeStruct((devices * lines, LANES), f32),
        ),
        in_specs=[
            vmem,
            pl.BlockSpec((chunk // LANES, LANES), lambda h: (h, 0)),
            pl.BlockSpec((cols, chunk), lambda h: (0, h)),
            pl.BlockSpec((chunk // LANES, LANES), lambda h: (h, 0)),
        ],
        out_specs=(vmem, vmem),
        scratch_shapes=[
            pltpu.VMEM((mids, HIGH * SLOT, LINE), f32),
            pltpu.VMEM((rows * SLOT // LANES, LANES), f32),
            pltpu.VMEM((LINE, 2 * LINE), jnp.bfloat16),
            pltpu.VMEM((LANES, 2 * LANES), jnp.bfloat16),
            pltpu.VMEM((devices, lines, LANES), jnp.int32),
            pltpu.SMEM((lines, LANES), jnp.int32),
            pltpu.SMEM((lines, LANES), jnp.int32),
            pltpu.VMEM((per_dev, LANES), f32),
            pltpu.VMEM((per_dev, LANES), f32),
            pltpu.SemaphoreType.DMA((2,)),
        ],
        compiler_params=pltpu.CompilerParams(vmem_limit_bytes=60 * 1024 * 1024),
    )(
        samples.reshape(devices, lines, LANES),
        sign_bits.reshape(-1, LANES),
        basis,
        target.reshape(-1, LANES),
    )

    half, chips = devices // 2, n_wide // 2
    copies = 2 * chips + 2 * (n_quad - 1) + n_wide - 1 + n_quad - 1
    flat = (cols + 8, GROUPS * cols)
    spaces = [
        (half, cols, per_dev), (half * lines, LANES),
        (half, cols, per_dev), (half * lines, LANES),
        (chips - 1, n_quad, cols, per_dev), (chips - 1, n_quad * lines, LANES),
        (n_quad, cols, per_dev), (n_quad * lines, LANES),
        (n_quad - 1, cols, per_dev), (n_quad - 1, n_quad * lines, LANES),
        (n_wide, *flat), flat, (n_quad - 1, *flat),
    ]
    sketch, gram = pl.pallas_call(
        functools.partial(reduce_kernel, n_wide, n_quad, total_samples),
        out_shape=(
            jax.ShapeDtypeStruct((cols + 1, per_dev), f32),
            jax.ShapeDtypeStruct(flat, f32),
        ),
        in_specs=[vmem, vmem, vmem],
        out_specs=(vmem, vmem),
        scratch_shapes=[pltpu.VMEM(space, f32) for space in spaces]
        + [pltpu.SemaphoreType.DMA((copies,))] * 2,
        compiler_params=pltpu.CompilerParams(collective_id=0, has_side_effects=True),
    )(main, last, owners.reshape(devices, lines, LANES))
    sketch, gram = pl.pallas_call(
        functools.partial(finish_kernel, n_quad),
        out_shape=(
            jax.ShapeDtypeStruct((cols + 1, per_dev), f32),
            jax.ShapeDtypeStruct((GROUPS // n_quad, cols, cols + 1), f32),
        ),
        in_specs=[vmem, vmem],
        out_specs=(vmem, vmem),
        scratch_shapes=[pltpu.VMEM((GROUPS * cols, LANES), f32)],
    )(sketch, gram)
    return sketch.T, gram


def solution(mesh):
    placed = (P(None, ("wide", "quad")), P(("wide", "quad")), P(("wide", "quad")), P(), P())
    return jax.shard_map(
        functools.partial(shards, mesh.shape["wide"], mesh.shape["quad"]),
        mesh=mesh,
        in_specs=placed,
        out_specs=(P(("wide", "quad"), None), P("quad", None, None)),
        check_vma=False,
    )
```

time: 65.8 us -> 54.8 us (0.83)
  Pallas kernels: 62.2 us -> 53.8 us
  local copies, waits for them, and re-layouts: 2.67 us -> 0 us
    pallas_call x1, Pallas kernels: 31 us -> 25.5 us  [shards(): pl.pallas_call(functools.partial(reduce_kernel, n_wide, n_quad, total_sam...]
    pallas_call x1, Pallas kernels: 31.1 us -> 26.9 us  [shards(): pl.pallas_call(functools.partial(transform_kernel, n_wide, n_quad, scale)...]
    unnamed x2 -> x0, local copies, waits for them, and re-layouts: 2.67 us -> none
    pallas_call x0 -> x1, Pallas kernels: none -> 1.45 us  [shards(): pl.pallas_call(functools.partial(finish_kernel, n_quad), out_shape=(jax.S...]
where the time goes in v2:
time: 54.8 us; the launch traced here: 54.5 us
  Pallas kernels  53.8 us (98%)
  between operations  0.65 us (1%)
    pallas_call x1, Pallas kernels, shards(): pl.pallas_call(functools.partial(transform_kernel, n_wide, n_quad, scale)...  26.9 us
    pallas_call x1, Pallas kernels, shards(): pl.pallas_call(functools.partial(reduce_kernel, n_wide, n_quad, total_sam...  25.5 us
    pallas_call x1, Pallas kernels, shards(): pl.pallas_call(functools.partial(finish_kernel, n_quad), out_shape=(jax.S...  1.45 us

profile of v2, /device:TPU:0, one launch (start us, length us, event | category | flops | bytes accessed | tf_op | source)
XLA Modules:
  0.0 54.5 jit_solution(10211318488174703378)
XLA Ops:
  0.6 26.9 %shard_map.68 = (f32[32,16,256]{2,1,0:T(8,128)}, f32[64,128]{1,0:T(8,128)}) custom-call(s32[32,2,128]{2,1,0:T(2,128)} %bitcast.7, s32[512,128]{1,0:T(8,128)} %bitcast.5, f32[16,65536]{1,0:T(8,128)} %x.1, f32[512,128]{1,0:T(8,128)} %bitcast.6), custom_call_target="tpu_custom_call" | custom-call | tf_op jit(solution)/shard_map/pallas_call | solution.py:303
  27.5 25.5 %shard_map.69 = (f32[17,256]{1,0:T(8,128)}, f32[24,128]{1,0:T(8,128)}) custom-call(f32[32,16,256]{2,1,0:T(8,128)} %get-tuple-element.8.main, f32[64,128]{1,0:T(8,128)} %get-tuple-element.9.last, s32[32,2,128]{2,1,0:T(2,128)} %bitcast.8), custom_call_target="tpu_custom_call" | custom-call | tf_op jit(solution)/shard_map/pallas_call | solution.py:348
  53.0 1.4 %shard_map.70 = (f32[17,256]{1,0:T(8,128)}, f32[2,16,17]{2,1,0:T(8,128)}) custom-call(f32[17,256]{1,0:T(8,128)} %get-tuple-element.10.sketch_in, f32[24,128]{1,0:T(8,128)} %get-tuple-element.11.gram_in), custom_call_target="tpu_custom_call" | custom-call | tf_op jit(solution)/shard_map/pallas_call | solution.py:360

commit v3 on v2

v3 whole, which is shorter than its diff:
```python
import functools
import math

import jax
import jax.numpy as jnp
from jax import lax
from jax.experimental import pallas as pl
from jax.experimental.pallas import tpu as pltpu
from jax.sharding import PartitionSpec as P

GROUPS = 8
LANES = 128
LINE = 256
HIGH = 8
SLOT = 32
MESH = pl.DeviceIdType.MESH


def bits_of(n):
    return n.bit_length() - 1


def parity(x, nbits):
    shift = 1
    while shift < nbits:
        x = x ^ (x >> shift)
        shift *= 2
    return x & 1


def butterfly(parts):
    half = 1
    while half < len(parts):
        for at in range(0, len(parts), 2 * half):
            for i in range(at, at + half):
                parts[i], parts[i + half] = parts[i] + parts[i + half], parts[i] - parts[i + half]
        half *= 2
    return parts


def place_of(high):
    return ((high & 1) * (HIGH // 2) + (high >> 1)) * SLOT


def split(x):
    top = x.astype(jnp.bfloat16)
    return top, (x - top.astype(jnp.float32)).astype(jnp.bfloat16)


def contract_last(a, b, **kw):
    return lax.dot_general(a, b, (((1,), (1,)), ((), ())), preferred_element_type=jnp.float32, **kw)


def sketch_kernel(
    n_wide, n_quad, scale, samp, owners, bits, x, t, sketch, gram,
    field, table, walsh, unit, picks, picks_a, picks_b, rows_a, rows_b, sems,
    main, last, got_main, got_last, sum_main, sum_last, wide_main, wide_last,
    row_main, row_last, quad_main, quad_last, wide_gram, own_gram, quad_gram,
    mate_sends, mate_recvs, chip_sends, chip_recvs, sends, recvs
):
    high = pl.program_id(0)
    chunk = x.shape[1]
    mids = chunk // LINE
    local_bits = bits_of(HIGH * chunk)
    devices, cols, per_dev = main.shape
    lines = per_dev // LANES
    wide = lax.axis_index("wide")
    quad = lax.axis_index("quad")
    me = wide * n_quad + quad
    core, chip, chips = wide % 2, wide // 2, n_wide // 2
    mate = (wide + 1 - 2 * core, quad)
    wide_peers = [((wide + k) % n_wide, quad) for k in range(1, n_wide)]
    quad_peers = [(wide, (quad + k) % n_quad) for k in range(1, n_quad)]
    barrier = pltpu.get_barrier_semaphore()

    @pl.when(high == 0)
    def _():
        for peer in wide_peers + quad_peers:
            pl.semaphore_signal(barrier, inc=1, device_id=peer, device_id_type=MESH)
        a = lax.broadcasted_iota(jnp.int32, (LINE, LINE), 0)
        b = lax.broadcasted_iota(jnp.int32, (LINE, LINE), 1)
        line = (1 - 2 * parity(a & b, bits_of(LINE))).astype(jnp.float32).astype(jnp.bfloat16)
        walsh[:, :LINE] = line
        walsh[:, LINE:] = line
        a = lax.broadcasted_iota(jnp.int32, (LANES, LANES), 0)
        b = lax.broadcasted_iota(jnp.int32, (LANES, LANES), 1)
        line = jnp.where(a == b, 1.0, 0.0).astype(jnp.bfloat16)
        unit[:, :LANES] = line
        unit[:, LANES:] = line
        picks[...] = samp[...] & (table.shape[0] - 1)

    row = lax.broadcasted_iota(jnp.int32, (8, LANES), 0)
    base = pl.multiple_of(place_of(high), SLOT)
    for part in range(LINE // LANES):
        for tile in range(cols // 8 + 1):
            values = []
            for mid in range(mids):
                line = mid * (LINE // LANES) + part
                flip = (1 - 2 * bits[line : line + 1, :]).astype(jnp.float32)
                if tile < cols // 8:
                    value = x[tile * 8 : tile * 8 + 8, line * LANES : (line + 1) * LANES] * flip
                else:
                    value = jnp.where(row == 0, t[line : line + 1, :] * flip, 0.0)
                values.append(value)
            for mid, value in enumerate(butterfly(values)):
                field[mid, pl.ds(base + tile * 8, 8), part * LANES : (part + 1) * LANES] = value

    @pl.when(high == HIGH - 1)
    def _():
        used = cols + 8

        def mix(mid, carry):
            halves = []
            for part in range(LINE // LANES):
                values = [
                    field[mid, place_of(h) : place_of(h) + used, part * LANES : (part + 1) * LANES]
                    for h in range(HIGH)
                ]
                values = butterfly(values)
                order = sorted(range(HIGH), key=place_of)
                blank = jnp.zeros((SLOT - used, LANES), jnp.float32)
                halves.append(jnp.concatenate([p for h in order for p in (values[h], blank)], axis=0))
            both = jnp.concatenate(split(jnp.concatenate(halves, axis=1)), axis=1)
            out = contract_last(walsh[...], both)
            at = pl.multiple_of(mid * LINE, LINE)
            table[pl.ds(at, LINE), :] = out[:, :LANES]
            table[pl.ds(at + mids * LINE, LINE), :] = out[:, LANES:]
            return carry

        lax.fori_loop(0, mids, mix, 0, unroll=2)
        table_rows = table.shape[0]
        half = devices // 2

        def chip_at(k):
            return (chip + 1 + k) % chips

        def device_at(slot):
            to_core = (core + 1 + slot // half) % 2
            to_wide = chip_at(slot // n_quad % chips) * 2 + to_core
            return to_wide * n_quad + slot % n_quad

        def fetch(slot, slots, sem):
            slot = jnp.minimum(slot, devices - 1)
            return pltpu.make_async_copy(picks.at[device_at(slot)], slots, sems.at[sem])

        def gather(slots, rows):
            for r in range(per_dev):
                rows[r : r + 1, :] = table[pl.ds(slots[r // LANES, r % LANES], 1), :]

        def finish(slot, rows):
            dev = device_at(slot)
            out = contract_last(unit[...], jnp.concatenate(split(rows[...]), axis=1))
            number = jnp.concatenate([samp[dev, i : i + 1] for i in range(lines)], axis=1)
            group = (number >> bits_of(table_rows)) & (LANES // SLOT - 1)
            sign = parity((number >> local_bits) & me, bits_of(devices))
            sign = (1 - 2 * sign).astype(jnp.float32) * scale
            total = jnp.zeros((used, per_dev), jnp.float32)
            for g in range(LANES // SLOT):
                total = jnp.where(group == g, out[g * SLOT : g * SLOT + used, :], total)
            total = total * sign
            main[slot] = total[:cols]
            for i in range(lines):
                last[pl.ds(slot * lines + i, 1), :] = total[cols : cols + 1, i * LANES : (i + 1) * LANES]

        def remote(src, dst, send_sem, recv_sem, peer):
            return pltpu.make_async_remote_copy(
                src_ref=src, dst_ref=dst, send_sem=send_sem, recv_sem=recv_sem,
                device_id=peer, device_id_type=MESH,
            )

        tall = n_quad * lines

        def group_of(k):
            return pl.ds(k * n_quad, n_quad), pl.ds(pl.multiple_of(k * tall, 8), tall)

        def mate_copies(k):
            at, at_last = group_of(k)
            return (
                remote(main.at[at], got_main.at[at], mate_sends.at[k], mate_recvs.at[k], mate),
                remote(
                    last.at[at_last], got_last.at[at_last],
                    mate_sends.at[chips + k], mate_recvs.at[chips + k], mate,
                ),
            )

        def chip_copies(k):
            at, at_last = group_of(k)
            peer = (chip_at(k) * 2 + core, quad)
            return (
                remote(sum_main.at[at], wide_main.at[k], chip_sends.at[k], chip_recvs.at[k], peer),
                remote(
                    sum_last.at[at_last], wide_last.at[k],
                    chip_sends.at[chips + k], chip_recvs.at[chips + k], peer,
                ),
            )

        fetch(0, picks_a, 0).start()
        fetch(1, picks_b, 1).start()
        fetch(0, picks_a, 0).wait()
        gather(picks_a, rows_a)
        fetch(2, picks_a, 0).start()
        pl.semaphore_wait(barrier, len(wide_peers) + len(quad_peers))

        def pair(i, carry):
            slot = 2 * i
            fetch(slot + 1, picks_b, 1).wait()
            gather(picks_b, rows_b)
            finish(slot, rows_a)
            fetch(slot + 3, picks_b, 1).start()
            fetch(slot + 2, picks_a, 0).wait()
            gather(picks_a, rows_a)
            finish(slot + 1, rows_b)
            fetch(slot + 4, picks_a, 0).start()
            return carry

        def step(k, carry):
            lax.fori_loop(k * n_quad // 2, (k + 1) * n_quad // 2, pair, 0)

            @pl.when(k < chips)
            def _():
                for copy in mate_copies(k):
                    copy.start()

            @pl.when(k >= chips)
            def _():
                own = k - chips
                for copy in mate_copies(own):
                    copy.wait_recv()
                at, at_last = group_of(own)
                from_at, from_last = group_of(k)
                sum_main[at] = main[from_at] + got_main[at]
                sum_last[at_last, :] = last[from_last, :] + got_last[at_last, :]

                @pl.when(own < chips - 1)
                def _():
                    for copy in chip_copies(own):
                        copy.start()

            return carry

        lax.fori_loop(0, 2 * chips, step, 0)
        fetch(0, picks_a, 0).wait()
        fetch(0, picks_b, 1).wait()
        for k in range(chips):
            for copy in mate_copies(k):
                copy.wait_send()
        for k in range(chips - 1):
            for copy in chip_copies(k):
                copy.wait()

        def add_row(to):
            row = sum_main[(chips - 1) * n_quad + to]
            for k in range(chips - 1):
                row = row + wide_main[k, to]
            row_main[to] = row

        sem_at = [0]

        def send(src, dst, peer):
            sem = sem_at[0]
            sem_at[0] += 1
            copy = remote(src, dst, sends.at[sem], recvs.at[sem], peer)
            copy.start()
            return copy

        ends = sum_last[(chips - 1) * tall :, :]
        for k in range(chips - 1):
            ends = ends + wide_last[k]
        row_last[...] = ends
        copies = []
        for k, peer in enumerate(quad_peers):
            add_row(peer[1])
            copies.append(send(row_main.at[peer[1]], quad_main.at[k], peer))
            copies.append(send(row_last, quad_last.at[k], peer))
        add_row(quad)
        for copy in copies:
            copy.wait()
        total = row_main[quad]
        ends = [row_last[pl.ds(quad * lines + i, 1), :] for i in range(lines)]
        for k in range(n_quad - 1):
            total = total + quad_main[k]
            ends = [e + quad_last[k, pl.ds(quad * lines + i, 1), :] for i, e in enumerate(ends)]
        end = jnp.concatenate(ends, axis=1)
        sketch[:cols, :] = total
        sketch[cols : cols + 1, :] = end

        group = jnp.concatenate([owners[me, i : i + 1] for i in range(lines)], axis=1)
        first = lax.broadcasted_iota(jnp.int32, (8, per_dev), 0) == 0
        right = jnp.concatenate([total, jnp.where(first, end, 0.0)], axis=0)
        left = jnp.concatenate([jnp.where(group == g, total, 0.0) for g in range(GROUPS)], axis=0)
        part = contract_last(right, left, precision=lax.Precision.HIGHEST)
        wide_gram[0] = part * (GROUPS / (per_dev * devices))
        copies = [send(wide_gram.at[0], wide_gram.at[k + 1], peer) for k, peer in enumerate(wide_peers)]
        for copy in copies:
            copy.wait()
        part = wide_gram[wide]
        for w in range(1, n_wide):
            part = part + wide_gram[(wide + n_wide - w) % n_wide]
        own_gram[...] = part
        copies = [send(own_gram, quad_gram.at[k], peer) for k, peer in enumerate(quad_peers)]
        for copy in copies:
            copy.wait()
        for k in range(n_quad - 1):
            part = part + quad_gram[k]
        gram[...] = part


def finish_kernel(n_quad, sketch_in, gram_in, sketch, gram, turned):
    quad = lax.axis_index("quad")
    owned, cols, _ = gram.shape
    sketch[...] = sketch_in[...]
    turned[:, : gram_in.shape[0]] = gram_in[...].T
    for g in range(owned):
        gram[g] = turned[pl.ds((quad * owned + g) * cols, cols), : cols + 1]


def shards(n_wide, n_quad, basis, target, sign_bits, samples, owners):
    cols, rows = basis.shape
    devices = n_wide * n_quad
    total_samples = samples.shape[0]
    per_dev = total_samples // devices
    lines = per_dev // LANES
    scale = 1.0 / math.sqrt(rows * devices)
    chunk = rows // HIGH
    mids = chunk // LINE
    vmem = pl.BlockSpec(memory_space=pltpu.VMEM)
    f32 = jnp.float32
    half, chips = devices // 2, n_wide // 2
    flat = (cols + 8, GROUPS * cols)
    spaces = [
        (devices, cols, per_dev), (devices * lines, LANES),
        (half, cols, per_dev), (half * lines, LANES),
        (half, cols, per_dev), (half * lines, LANES),
        (chips - 1, n_quad, cols, per_dev), (chips - 1, n_quad * lines, LANES),
        (n_quad, cols, per_dev), (n_quad * lines, LANES),
        (n_quad - 1, cols, per_dev), (n_quad - 1, n_quad * lines, LANES),
        (n_wide, *flat), flat, (n_quad - 1, *flat),
    ]
    copies = [2 * chips, 2 * chips, 3 * (n_quad - 1) + n_wide - 1]
    sketch, gram = pl.pallas_call(
        functools.partial(sketch_kernel, n_wide, n_quad, scale),
        grid=(HIGH,),
        out_shape=(
            jax.ShapeDtypeStruct((cols + 1, per_dev), f32),
            jax.ShapeDtypeStruct(flat, f32),
        ),
        in_specs=[
            vmem,
            vmem,
            pl.BlockSpec((chunk // LANES, LANES), lambda h: (h, 0)),
            pl.BlockSpec((cols, chunk), lambda h: (0, h)),
            pl.BlockSpec((chunk // LANES, LANES), lambda h: (h, 0)),
        ],
        out_specs=(vmem, vmem),
        scratch_shapes=[
            pltpu.VMEM((mids, HIGH * SLOT, LINE), f32),
            pltpu.VMEM((rows * SLOT // LANES, LANES), f32),
            pltpu.VMEM((LINE, 2 * LINE), jnp.bfloat16),
            pltpu.VMEM((LANES, 2 * LANES), jnp.bfloat16),
            pltpu.VMEM((devices, lines, LANES), jnp.int32),
            pltpu.SMEM((lines, LANES), jnp.int32),
            pltpu.SMEM((lines, LANES), jnp.int32),
            pltpu.VMEM((per_dev, LANES), f32),
            pltpu.VMEM((per_dev, LANES), f32),
            pltpu.SemaphoreType.DMA((2,)),
        ]
        + [pltpu.VMEM(space, f32) for space in spaces]
        + [pltpu.SemaphoreType.DMA((n,)) for n in copies for _ in range(2)],
        compiler_params=pltpu.CompilerParams(
            vmem_limit_bytes=60 * 1024 * 1024, collective_id=0, has_side_effects=True
        ),
    )(
        samples.reshape(devices, lines, LANES),
        owners.reshape(devices, lines, LANES),
        sign_bits.reshape(-1, LANES),
        basis,
        target.reshape(-1, LANES),
    )
    sketch, gram = pl.pallas_call(
        functools.partial(finish_kernel, n_quad),
        out_shape=(
            jax.ShapeDtypeStruct((cols + 1, per_dev), f32),
            jax.ShapeDtypeStruct((GROUPS // n_quad, cols, cols + 1), f32),
        ),
        in_specs=[vmem, vmem],
        out_specs=(vmem, vmem),
        scratch_shapes=[pltpu.VMEM((GROUPS * cols, LANES), f32)],
    )(sketch, gram)
    return sketch.T, gram


def solution(mesh):
    placed = (P(None, ("wide", "quad")), P(("wide", "quad")), P(("wide", "quad")), P(), P())
    return jax.shard_map(
        functools.partial(shards, mesh.shape["wide"], mesh.shape["quad"]),
        mesh=mesh,
        in_specs=placed,
        out_specs=(P(("wide", "quad"), None), P("quad", None, None)),
        check_vma=False,
    )
```

time: 54.8 us -> 45.3 us (0.83)
  Pallas kernels: 53.8 us -> 44.3 us
    pallas_call x2 -> x1, Pallas kernels: 52.4 us -> 42.9 us  [shards(): pl.pallas_call(functools.partial(sketch_kernel, n_wide, n_quad, scale), g...]
where the time goes in v3:
time: 45.3 us; the launch traced here: 45 us
  Pallas kernels  44.3 us (98%)
  between operations  0.64 us (1%)
    pallas_call x1, Pallas kernels, shards(): pl.pallas_call(functools.partial(sketch_kernel, n_wide, n_quad, scale), g...  42.9 us
    pallas_call x1, Pallas kernels, shards(): pl.pallas_call(functools.partial(finish_kernel, n_quad), out_shape=(jax.S...  1.45 us

profile of v3, /device:TPU:0, one launch (start us, length us, event | category | flops | bytes accessed | tf_op | source)
XLA Modules:
  0.0 45.0 jit_solution(5749626732979888638)
XLA Ops:
  0.6 42.9 %shard_map.68 = (f32[17,256]{1,0:T(8,128)}, f32[24,128]{1,0:T(8,128)}) custom-call(s32[32,2,128]{2,1,0:T(2,128)} %bitcast.7, s32[32,2,128]{2,1,0:T(2,128)} %bitcast.8, s32[512,128]{1,0:T(8,128)} %bitcast.5, f32[16,65536]{1,0:T(8,128)} %x.1, f32[512,128]{1,0:T(8,128)} %bitcast.6), custom_call_target="tpu_custom_call" | custom-call | tf_op jit(solution)/shard_map/pallas_call | solution.py:340
  43.5 1.4 %shard_map.69 = (f32[17,256]{1,0:T(8,128)}, f32[2,16,17]{2,1,0:T(8,128)}) custom-call(f32[17,256]{1,0:T(8,128)} %get-tuple-element.6.sketch_in, f32[24,128]{1,0:T(8,128)} %get-tuple-element.7.gram_in), custom_call_target="tpu_custom_call" | custom-call | tf_op jit(solution)/shard_map/pallas_call | solution.py:379

commit v4 on v0

v4 whole, which is shorter than its diff:
```python
import functools
import math

import jax
import jax.numpy as jnp
from jax import lax
from jax.experimental import pallas as pl
from jax.experimental.pallas import tpu as pltpu
from jax.sharding import PartitionSpec as P

GROUPS = 8
LANES = 128
LINE = 256
HIGH = 8
SLOT = 32
MESH = pl.DeviceIdType.MESH


def bits_of(n):
    return n.bit_length() - 1


def parity(x, nbits):
    shift = 1
    while shift < nbits:
        x = x ^ (x >> shift)
        shift *= 2
    return x & 1


def butterfly(parts):
    half = 1
    while half < len(parts):
        for at in range(0, len(parts), 2 * half):
            for i in range(at, at + half):
                parts[i], parts[i + half] = parts[i] + parts[i + half], parts[i] - parts[i + half]
        half *= 2
    return parts


def place_of(high):
    return ((high & 1) * (HIGH // 2) + (high >> 1)) * SLOT


def split(x):
    top = x.astype(jnp.bfloat16)
    return top, (x - top.astype(jnp.float32)).astype(jnp.bfloat16)


def contract_last(a, b, **kw):
    return lax.dot_general(a, b, (((1,), (1,)), ((), ())), preferred_element_type=jnp.float32, **kw)


def sketch_kernel(
    n_wide, n_quad, scale, samp, owners, bits_in, x_in, t_in, sketch, gram,
    bits_all, x_all, t_all, load_sems,
    field, table, walsh, unit, picks, picks_a, picks_b, rows_a, rows_b, sems,
    main, last, got_main, got_last, sum_main, sum_last, wide_main, wide_last,
    row_main, row_last, quad_main, quad_last, wide_gram, own_gram, quad_gram,
    mate_sends, mate_recvs, chip_sends, chip_recvs, sends, recvs
):
    chunk = x_all.shape[2]
    lines_in = chunk // LANES
    mids = chunk // LINE
    local_bits = bits_of(HIGH * chunk)
    devices, cols, per_dev = main.shape
    lines = per_dev // LANES
    wide = lax.axis_index("wide")
    quad = lax.axis_index("quad")
    me = wide * n_quad + quad
    core, chip, chips = wide % 2, wide // 2, n_wide // 2
    mate = (wide + 1 - 2 * core, quad)
    wide_peers = [((wide + k) % n_wide, quad) for k in range(1, n_wide)]
    quad_peers = [(wide, (quad + k) % n_quad) for k in range(1, n_quad)]
    barrier = pltpu.get_barrier_semaphore()

    def loads(h):
        at = pl.multiple_of(h * chunk, chunk)
        rows = pl.ds(pl.multiple_of(h * lines_in, lines_in), lines_in)
        return (
            pltpu.make_async_copy(bits_in.at[rows], bits_all.at[h], load_sems.at[0, h]),
            pltpu.make_async_copy(t_in.at[rows], t_all.at[h], load_sems.at[1, h]),
            pltpu.make_async_copy(x_in.at[:, pl.ds(at, chunk)], x_all.at[h], load_sems.at[2, h]),
        )

    for h in range(HIGH):
        for copy in loads(h):
            copy.start()
    for peer in wide_peers + quad_peers:
        pl.semaphore_signal(barrier, inc=1, device_id=peer, device_id_type=MESH)
    a = lax.broadcasted_iota(jnp.int32, (LINE, LINE), 0)
    b = lax.broadcasted_iota(jnp.int32, (LINE, LINE), 1)
    line = (1 - 2 * parity(a & b, bits_of(LINE))).astype(jnp.float32).astype(jnp.bfloat16)
    walsh[:, :LINE] = line
    walsh[:, LINE:] = line
    a = lax.broadcasted_iota(jnp.int32, (LANES, LANES), 0)
    b = lax.broadcasted_iota(jnp.int32, (LANES, LANES), 1)
    line = jnp.where(a == b, 1.0, 0.0).astype(jnp.bfloat16)
    unit[:, :LANES] = line
    unit[:, LANES:] = line
    picks[...] = samp[...] & (table.shape[0] - 1)

    row = lax.broadcasted_iota(jnp.int32, (8, LANES), 0)

    def first_pass(high, carry):
        for copy in loads(high):
            copy.wait()
        bits, t, x = bits_all.at[high], t_all.at[high], x_all.at[high]
        base = pl.multiple_of(place_of(high), SLOT)
        for part in range(LINE // LANES):
            for tile in range(cols // 8 + 1):
                values = []
                for mid in range(mids):
                    line = mid * (LINE // LANES) + part
                    flip = (1 - 2 * bits[line : line + 1, :]).astype(jnp.float32)
                    if tile < cols // 8:
                        value = x[tile * 8 : tile * 8 + 8, line * LANES : (line + 1) * LANES] * flip
                    else:
                        value = jnp.where(row == 0, t[line : line + 1, :] * flip, 0.0)
                    values.append(value)
                for mid, value in enumerate(butterfly(values)):
                    field[mid, pl.ds(base + tile * 8, 8), part * LANES : (part + 1) * LANES] = value
        return carry

    lax.fori_loop(0, HIGH, first_pass, 0)
    used = cols + 8

    def mix(mid, carry):
        halves = []
        for part in range(LINE // LANES):
            values = [
                field[mid, place_of(h) : place_of(h) + used, part * LANES : (part + 1) * LANES]
                for h in range(HIGH)
            ]
            values = butterfly(values)
            order = sorted(range(HIGH), key=place_of)
            blank = jnp.zeros((SLOT - used, LANES), jnp.float32)
            halves.append(jnp.concatenate([p for h in order for p in (values[h], blank)], axis=0))
        both = jnp.concatenate(split(jnp.concatenate(halves, axis=1)), axis=1)
        out = contract_last(walsh[...], both)
        at = pl.multiple_of(mid * LINE, LINE)
        table[pl.ds(at, LINE), :] = out[:, :LANES]
        table[pl.ds(at + mids * LINE, LINE), :] = out[:, LANES:]
        return carry

    lax.fori_loop(0, mids, mix, 0, unroll=4)
    table_rows = table.shape[0]
    half = devices // 2

    def chip_at(k):
        return (chip + 1 + k) % chips

    def device_at(slot):
        to_core = (core + 1 + slot // half) % 2
        to_wide = chip_at(slot // n_quad % chips) * 2 + to_core
        return to_wide * n_quad + slot % n_quad

    def fetch(slot, slots, sem):
        slot = jnp.minimum(slot, devices - 1)
        return pltpu.make_async_copy(picks.at[device_at(slot)], slots, sems.at[sem])

    def gather(slots, rows):
        for r in range(per_dev):
            rows[r : r + 1, :] = table[pl.ds(slots[r // LANES, r % LANES], 1), :]

    def finish(slot, rows):
        dev = device_at(slot)
        out = contract_last(unit[...], jnp.concatenate(split(rows[...]), axis=1))
        number = jnp.concatenate([samp[dev, i : i + 1] for i in range(lines)], axis=1)
        group = (number >> bits_of(table_rows)) & (LANES // SLOT - 1)
        sign = parity((number >> local_bits) & me, bits_of(devices))
        sign = (1 - 2 * sign).astype(jnp.float32) * scale
        total = jnp.zeros((used, per_dev), jnp.float32)
        for g in range(LANES // SLOT):
            total = jnp.where(group == g, out[g * SLOT : g * SLOT + used, :], total)
        total = total * sign
        main[slot] = total[:cols]
        for i in range(lines):
            last[pl.ds(slot * lines + i, 1), :] = total[cols : cols + 1, i * LANES : (i + 1) * LANES]

    def remote(src, dst, send_sem, recv_sem, peer):
        return pltpu.make_async_remote_copy(
            src_ref=src, dst_ref=dst, send_sem=send_sem, recv_sem=recv_sem,
            device_id=peer, device_id_type=MESH,
        )

    tall = n_quad * lines

    def group_of(k):
        return pl.ds(k * n_quad, n_quad), pl.ds(pl.multiple_of(k * tall, 8), tall)

    def mate_copies(k):
        at, at_last = group_of(k)
        return (
            remote(main.at[at], got_main.at[at], mate_sends.at[k], mate_recvs.at[k], mate),
            remote(
                last.at[at_last], got_last.at[at_last],
                mate_sends.at[chips + k], mate_recvs.at[chips + k], mate,
            ),
        )

    def chip_copies(k):
        at, at_last = group_of(k)
        peer = (chip_at(k) * 2 + core, quad)
        return (
            remote(sum_main.at[at], wide_main.at[k], chip_sends.at[k], chip_recvs.at[k], peer),
            remote(
                sum_last.at[at_last], wide_last.at[k],
                chip_sends.at[chips + k], chip_recvs.at[chips + k], peer,
            ),
        )

    fetch(0, picks_a, 0).start()
    fetch(1, picks_b, 1).start()
    fetch(0, picks_a, 0).wait()
    gather(picks_a, rows_a)
    fetch(2, picks_a, 0).start()
    pl.semaphore_wait(barrier, len(wide_peers) + len(quad_peers))

    def pair(i, carry):
        slot = 2 * i
        fetch(slot + 1, picks_b, 1).wait()
        gather(picks_b, rows_b)
        finish(slot, rows_a)
        fetch(slot + 3, picks_b, 1).start()
        fetch(slot + 2, picks_a, 0).wait()
        gather(picks_a, rows_a)
        finish(slot + 1, rows_b)
        fetch(slot + 4, picks_a, 0).start()
        return carry

    def step(k, carry):
        lax.fori_loop(k * n_quad // 2, (k + 1) * n_quad // 2, pair, 0)

        @pl.when(k < chips)
        def _():
            for copy in mate_copies(k):
                copy.start()

        @pl.when(k >= chips)
        def _():
            own = k - chips
            for copy in mate_copies(own):
                copy.wait_recv()
            at, at_last = group_of(own)
            from_at, from_last = group_of(k)
            sum_main[at] = main[from_at] + got_main[at]
            sum_last[at_last, :] = last[from_last, :] + got_last[at_last, :]

            @pl.when(own < chips - 1)
            def _():
                for copy in chip_copies(own):
                    copy.start()

        return carry

    lax.fori_loop(0, 2 * chips, step, 0)
    fetch(0, picks_a, 0).wait()
    fetch(0, picks_b, 1).wait()
    for k in range(chips):
        for copy in mate_copies(k):
            copy.wait_send()
    for k in range(chips - 1):
        for copy in chip_copies(k):
            copy.wait()

    def add_row(to):
        row = sum_main[(chips - 1) * n_quad + to]
        for k in range(chips - 1):
            row = row + wide_main[k, to]
        row_main[to] = row

    sem_at = [0]

    def send(src, dst, peer):
        sem = sem_at[0]
        sem_at[0] += 1
        copy = remote(src, dst, sends.at[sem], recvs.at[sem], peer)
        copy.start()
        return copy

    ends = sum_last[(chips - 1) * tall :, :]
    for k in range(chips - 1):
        ends = ends + wide_last[k]
    row_last[...] = ends
    copies = []
    for k, peer in enumerate(quad_peers):
        add_row(peer[1])
        copies.append(send(row_main.at[peer[1]], quad_main.at[k], peer))
        copies.append(send(row_last, quad_last.at[k], peer))
    add_row(quad)
    for copy in copies:
        copy.wait()
    total = row_main[quad]
    ends = [row_last[pl.ds(quad * lines + i, 1), :] for i in range(lines)]
    for k in range(n_quad - 1):
        total = total + quad_main[k]
        ends = [e + quad_last[k, pl.ds(quad * lines + i, 1), :] for i, e in enumerate(ends)]
    end = jnp.concatenate(ends, axis=1)
    sketch[:cols, :] = total
    sketch[cols : cols + 1, :] = end

    group = jnp.concatenate([owners[me, i : i + 1] for i in range(lines)], axis=1)
    first = lax.broadcasted_iota(jnp.int32, (8, per_dev), 0) == 0
    right = jnp.concatenate([total, jnp.where(first, end, 0.0)], axis=0)
    left = jnp.concatenate([jnp.where(group == g, total, 0.0) for g in range(GROUPS)], axis=0)
    part = contract_last(right, left, precision=lax.Precision.HIGHEST)
    part = part * (GROUPS / (per_dev * devices))
    span = GROUPS * cols // n_quad
    block = lax.broadcasted_iota(jnp.int32, (8, LANES), 1) // span
    for q in range(n_quad):
        packed = jnp.zeros((8, LANES), jnp.float32)
        for tile in range(part.shape[0] // 8):
            turned = part[tile * 8 : tile * 8 + 8, :]
            if (tile - q) % n_quad:
                turned = pltpu.roll(turned, (tile - q) % n_quad * span, 1)
            packed = jnp.where(block == tile, turned, packed)
        own_gram[q] = packed
    copies = [send(own_gram.at[peer[1]], quad_gram.at[k], peer) for k, peer in enumerate(quad_peers)]
    for copy in copies:
        copy.wait()
    packed = own_gram[quad]
    for k in range(n_quad - 1):
        packed = packed + quad_gram[k]
    wide_gram[0] = packed
    copies = [send(wide_gram.at[0], wide_gram.at[k + 1], peer) for k, peer in enumerate(wide_peers)]
    for copy in copies:
        copy.wait()
    packed = wide_gram[wide]
    for w in range(1, n_wide):
        packed = packed + wide_gram[(wide + n_wide - w) % n_wide]
    gram[...] = packed


def finish_kernel(sketch_in, gram_in, sketch, gram):
    owned, cols, width = gram.shape
    sketch[...] = sketch_in[...]
    turned = gram_in[...].T
    for tile in range(-(-width // 8)):
        columns = min(8, width - tile * 8)
        for g in range(owned):
            at = (tile * owned + g) * cols
            gram[g, :, tile * 8 : tile * 8 + columns] = turned[at : at + cols, :columns]


def shards(n_wide, n_quad, basis, target, sign_bits, samples, owners):
    cols, rows = basis.shape
    devices = n_wide * n_quad
    total_samples = samples.shape[0]
    per_dev = total_samples // devices
    lines = per_dev // LANES
    scale = 1.0 / math.sqrt(rows * devices)
    chunk = rows // HIGH
    mids = chunk // LINE
    vmem = pl.BlockSpec(memory_space=pltpu.VMEM)
    f32 = jnp.float32
    half, chips = devices // 2, n_wide // 2
    flat = (8, LANES)
    spaces = [
        (devices, cols, per_dev), (devices * lines, LANES),
        (half, cols, per_dev), (half * lines, LANES),
        (half, cols, per_dev), (half * lines, LANES),
        (chips - 1, n_quad, cols, per_dev), (chips - 1, n_quad * lines, LANES),
        (n_quad, cols, per_dev), (n_quad * lines, LANES),
        (n_quad - 1, cols, per_dev), (n_quad - 1, n_quad * lines, LANES),
        (n_wide, *flat), (n_quad, *flat), (n_quad - 1, *flat),
    ]
    copies = [2 * chips, 2 * chips, 3 * (n_quad - 1) + n_wide - 1]
    sketch, gram = pl.pallas_call(
        functools.partial(sketch_kernel, n_wide, n_quad, scale),
        out_shape=(
            jax.ShapeDtypeStruct((cols + 1, per_dev), f32),
            jax.ShapeDtypeStruct(flat, f32),
        ),
        in_specs=[
            vmem,
            vmem,
            pl.BlockSpec(memory_space=pl.ANY),
            pl.BlockSpec(memory_space=pl.ANY),
            pl.BlockSpec(memory_space=pl.ANY),
        ],
        out_specs=(vmem, vmem),
        scratch_shapes=[
            pltpu.VMEM((HIGH, chunk // LANES, LANES), jnp.int32),
            pltpu.VMEM((HIGH, cols, chunk), f32),
            pltpu.VMEM((HIGH, chunk // LANES, LANES), f32),
            pltpu.SemaphoreType.DMA((3, HIGH)),
            pltpu.VMEM((mids, HIGH * SLOT, LINE), f32),
            pltpu.VMEM((rows * SLOT // LANES, LANES), f32),
            pltpu.VMEM((LINE, 2 * LINE), jnp.bfloat16),
            pltpu.VMEM((LANES, 2 * LANES), jnp.bfloat16),
            pltpu.VMEM((devices, lines, LANES), jnp.int32),
            pltpu.SMEM((lines, LANES), jnp.int32),
            pltpu.SMEM((lines, LANES), jnp.int32),
            pltpu.VMEM((per_dev, LANES), f32),
            pltpu.VMEM((per_dev, LANES), f32),
            pltpu.SemaphoreType.DMA((2,)),
        ]
        + [pltpu.VMEM(space, f32) for space in spaces]
        + [pltpu.SemaphoreType.DMA((n,)) for n in copies for _ in range(2)],
        compiler_params=pltpu.CompilerParams(
            vmem_limit_bytes=60 * 1024 * 1024, collective_id=0, has_side_effects=True
        ),
    )(
        samples.reshape(devices, lines, LANES),
        owners.reshape(devices, lines, LANES),
        sign_bits.reshape(-1, LANES),
        basis,
        target.reshape(-1, LANES),
    )
    sketch, gram = pl.pallas_call(
        finish_kernel,
        out_shape=(
            jax.ShapeDtypeStruct((cols + 1, per_dev), f32),
            jax.ShapeDtypeStruct((GROUPS // n_quad, cols, cols + 1), f32),
        ),
        in_specs=[vmem, vmem],
        out_specs=(vmem, vmem),
    )(sketch, gram)
    return sketch.T, gram


def solution(mesh):
    placed = (P(None, ("wide", "quad")), P(("wide", "quad")), P(("wide", "quad")), P(), P())
    return jax.shard_map(
        functools.partial(shards, mesh.shape["wide"], mesh.shape["quad"]),
        mesh=mesh,
        in_specs=placed,
        out_specs=(P(("wide", "quad"), None), P("quad", None, None)),
        check_vma=False,
    )
```

time: 309 us -> 41.5 us (0.13)
  local copies, waits for them, and re-layouts: 124 us -> 0 us
  waiting for transfers between devices: 104 us -> 0 us
  Pallas kernels: 0 us -> 40.6 us
  blocking collectives: 39.6 us -> 0 us
  matrix products: 13.6 us -> 0 us
  between operations: 14.2 us -> 0.64 us
  other arithmetic: 12.7 us -> 0 us
    reduce_scatter x2 -> x0, waiting for transfers between devices: 104 us -> none  [the longest x1 67 us: shards(): lax.psum_scatter(values * sign[None, :], 'quad', scatter_dimension=1, til...]
    gather x3 -> x0, local copies, waits for them, and re-layouts: 95.6 us -> none  [the longest x1 45.5 us: shards(): number = samples[slots]]
    pallas_call x0 -> x2, Pallas kernels: none -> 40.6 us  [the longest x1 39.1 us: shards(): pl.pallas_call(functools.partial(sketch_kernel, n_wide, n_quad, scale), o...]
    psum x1 -> x0, blocking collectives: 39.6 us -> none  [shards(): summed = lax.psum(partial_gram, ('wide', 'quad'))]
    reshape x1 -> x0, local copies, waits for them, and re-layouts: 18 us -> none  [shards(): local = cube.reshape(width, rows)]
    dot_general x3 -> x0, matrix products: 13.6 us -> none  [the longest x1 6.72 us: shards(): jnp.einsum('kab,ac->kcb', cube, table, precision=lax.Precision.HIGHEST)]
    mul x3 -> x0, other arithmetic: 12.3 us -> none  [the longest x1 9.67 us: shards(): values * sign[None, :]]
    unnamed x7 -> x0, local copies, waits for them, and re-layouts: 7.58 us -> none
  transfers between devices with their start and end apart: 2 -> 0, of which waited for: 2 -> 0; matrix products, arithmetic and copies ran while one was open for 4% -> 0% of each run, Pallas kernels for 0% -> 0%
where the time goes in v4:
time: 41.5 us; the launch traced here: 41.3 us
  Pallas kernels  40.6 us (98%)
  between operations  0.64 us (2%)
    pallas_call x1, Pallas kernels, shards(): pl.pallas_call(functools.partial(sketch_kernel, n_wide, n_quad, scale), o...  39.1 us
    pallas_call x1, Pallas kernels, shards(): pl.pallas_call(finish_kernel, out_shape=(jax.ShapeDtypeStruct((cols + 1,...  1.51 us

profile of v4, /device:TPU:0, one launch (start us, length us, event | category | flops | bytes accessed | tf_op | source)
XLA Modules:
  0.0 41.3 jit_solution(13701189664440065084)
XLA Ops:
  0.6 39.1 %shard_map.68 = (f32[17,256]{1,0:T(8,128)}, f32[8,128]{1,0:T(8,128)}) custom-call(s32[32,2,128]{2,1,0:T(2,128)} %bitcast.7, s32[32,2,128]{2,1,0:T(2,128)} %bitcast.8, s32[512,128]{1,0:T(8,128)} %bitcast.5, f32[16,65536]{1,0:T(8,128)} %x_in.1, f32[512,128]{1,0:T(8,128)} %bitcast.6), custom_call_target="tpu_custom_call" | custom-call | tf_op jit(solution)/shard_map/pallas_call | solution.py:369
  39.8 1.5 %shard_map.69 = (f32[17,256]{1,0:T(8,128)}, f32[2,16,17]{2,1,0:T(8,128)}) custom-call(f32[17,256]{1,0:T(8,128)} %get-tuple-element.6.sketch_in, f32[8,128]{1,0:T(8,128)} %get-tuple-element.7.gram_in), custom_call_target="tpu_custom_call" | custom-call | tf_op jit(solution)/shard_map/pallas_call | solution.py:411

commit v5 on v4

--- a/solution.py
+++ b/solution.py
@@ -143,7 +143,7 @@
         table[pl.ds(at + mids * LINE, LINE), :] = out[:, LANES:]
         return carry
 
-    lax.fori_loop(0, mids, mix, 0, unroll=4)
+    lax.fori_loop(0, mids, mix, 0, unroll=8)
     table_rows = table.shape[0]
     half = devices // 2
 

time: 41.5 us -> 40.7 us (0.981)
  Pallas kernels: 40.6 us -> 39.9 us
    pallas_call x1, Pallas kernels: 39.1 us -> 38.4 us  [shards(): pl.pallas_call(functools.partial(sketch_kernel, n_wide, n_quad, scale), o...]
where the time goes in v5:
time: 40.7 us; the launch traced here: 40.5 us
  Pallas kernels  39.9 us (98%)
  between operations  0.64 us (2%)
    pallas_call x1, Pallas kernels, shards(): pl.pallas_call(functools.partial(sketch_kernel, n_wide, n_quad, scale), o...  38.4 us
    pallas_call x1, Pallas kernels, shards(): pl.pallas_call(finish_kernel, out_shape=(jax.ShapeDtypeStruct((cols + 1,...  1.51 us

profile of v5, /device:TPU:0, one launch (start us, length us, event | category | flops | bytes accessed | tf_op | source)
XLA Modules:
  0.0 40.5 jit_solution(12676602989429076532)
XLA Ops:
  0.6 38.4 %shard_map.68 = (f32[17,256]{1,0:T(8,128)}, f32[8,128]{1,0:T(8,128)}) custom-call(s32[32,2,128]{2,1,0:T(2,128)} %bitcast.7, s32[32,2,128]{2,1,0:T(2,128)} %bitcast.8, s32[512,128]{1,0:T(8,128)} %bitcast.5, f32[16,65536]{1,0:T(8,128)} %x_in.1, f32[512,128]{1,0:T(8,128)} %bitcast.6), custom_call_target="tpu_custom_call" | custom-call | tf_op jit(solution)/shard_map/pallas_call | solution.py:369
  39.0 1.5 %shard_map.69 = (f32[17,256]{1,0:T(8,128)}, f32[2,16,17]{2,1,0:T(8,128)}) custom-call(f32[17,256]{1,0:T(8,128)} %get-tuple-element.6.sketch_in, f32[8,128]{1,0:T(8,128)} %get-tuple-element.7.gram_in), custom_call_target="tpu_custom_call" | custom-call | tf_op jit(solution)/shard_map/pallas_call | solution.py:411
